TPU v7x, 256 devices: a whole 4x4x8 slice. The times are simulated.
256 devices in a mesh: dp: 2 (over z_hi), tensor: 4 (over y), pool: 32 (over x, z_lo, core).
Axes of the slice: x: 4, y: 4, z: 8 (z_hi: 2, z_lo: 4; z = z_hi * 4 + z_lo), core: 2. Of those that a mesh axis runs over, the one named last changes fastest.
Arguments:
- tokens: bfloat16 [64, 1024, 4096], P(('dp', 'pool')), may hold values from -192 to 192, as said below
- w_hidden: bfloat16 [4096, 4096], P('pool', 'tensor'), may hold values from -0.09375 to 0.09375
- w_out: bfloat16 [4096, 256], P('tensor'), may hold values from -0.09375 to 0.09375
- bank: bfloat16 [32768, 256], P('pool'), may hold values from -0.5 to 0.5
- item_ids: int32 [32768], P('pool'), may hold values from 0 to 1048575
- log_freq: bfloat16 [1048576], replicated, may hold values from -14 to -6
- positives: int32 [64, 1024], P(('dp', 'pool'), 'tensor'), may hold values from 0 to 32767
- new_items: bfloat16 [8192, 256], P('pool'), may hold values from -0.5 to 0.5
- new_owner: int32 [8192, 1], P('pool'), may hold values from 0 to 31; in each aligned block of 256 rows (0 to 255, 256 to 511, ...) at most 16 rows name the same one
- queue_head: int32 [32], P('pool'), may hold values from 0 to 1023
Outputs:
- query_loss: float32 [64, 1024], P(('dp', 'pool'), 'tensor')
- new_bank: bfloat16 [32768, 256], P('pool')
Inputs may be any that keep to these rules, and one draw needn't show every extreme that they name: `tokens`: float values within the range. `new_owner`: among the 256 new rows of one pool index, no shard is named by more than 16 rows, a bound that some block reaches.
All inputs are finite; a program needn't handle non-finite values.
Results may differ from a plain program's by a relative error of at most 0.002.
Values may be sent and summed in bfloat16 or wider, within the bound.
A program may use at most 128 MiB of HBM per device.

v0:
```python
import jax
import jax.numpy as jnp
from jax import lax
from jax.sharding import Mesh
from jax.sharding import PartitionSpec as P

POOL = ("pool_0", "pool_1", "pool_2")
DP_POOL = ("dp", "pool_0", "pool_1", "pool_2")
inv_temp = 5.0


def split_up(x, dim, count):
    before, after = (x.shape[:dim], x.shape[dim + 1 :])
    return jnp.moveaxis(x.reshape(*before, count, -1, *after), dim, 0)


def sum_at_owner(x, axis, dim):
    count = lax.axis_size(axis)
    blocks = lax.all_to_all(split_up(x, dim, count), axis, 0, 0, tiled=True)
    return jnp.sum(blocks, axis=0)


def all_in_one(x, axis):
    leaves = jax.tree.leaves(x)
    turns = sorted(range(len(leaves)), key=lambda k: -leaves[k].size)
    width = (1, *leaves[turns[0]].shape)[-1]
    lines = [
        jnp.pad(leaves[k].reshape(-1), (0, -leaves[k].size % width)).reshape(-1, width)
        for k in turns
    ]
    both, at, found = (lax.all_gather(jnp.concatenate(lines), axis), 0, {})
    for k, line in zip(turns, lines):
        section = both[:, at : at + len(line)].reshape(len(both), -1)
        found[k] = section[:, : leaves[k].size].reshape(-1, *leaves[k].shape)
        at += len(line)
    numbers = iter(range(len(leaves)))
    return jax.tree.map(lambda _: found[next(numbers)], x)


def joined_all(x, axes, combine):
    for axis in axes:
        pieces = all_in_one(x, axis)
        x = jax.tree.map(lambda part: part[0], pieces)
        for k in range(1, lax.axis_size(axis)):
            x = combine(x, jax.tree.map(lambda part: part[k], pieces))
    return x


def copy_for_each(x, axis):
    copies = jnp.broadcast_to(x, (lax.axis_size(axis), *x.shape))
    return lax.all_to_all(copies, axis, split_axis=0, concat_axis=0, tiled=True)


def folded_in_pairs(pieces, combine):
    while len(jax.tree.leaves(pieces)[0]) > 1:
        pieces = jax.vmap(combine)(*(pieces[side::2] for side in (0, 1)))
    return pieces[0]


def entering(x, axis, combine, identity):
    count, position = (lax.axis_size(axis), lax.axis_index(axis))
    passed = jnp.arange(count) < position

    def kept(part, zero, own):
        part = jnp.where(
            passed.reshape(-1, *(1 for _ in own.shape)), part, jnp.asarray(zero, own.dtype)
        )
        return part

    pieces = copy_for_each(x, axis)
    return folded_in_pairs(kept(pieces, identity, x), combine)


def local_stats(query_rows, target_rows, bank, offsets, base_column):
    row_count = query_rows.shape[0]
    bank_rows = bank.shape[0]
    block_width = 512
    block_count = bank_rows // block_width
    blocks = bank.reshape(block_count, block_width, bank.shape[1])
    shifts = offsets.reshape(block_count, block_width)

    def block_step(running, inputs):
        run_max, run_sum, run_pos = running
        bank_block, block_offsets, block_index = inputs
        logits = (
            inv_temp * jnp.dot(query_rows, bank_block.T, preferred_element_type=jnp.float32)
            - block_offsets[None, :]
        )
        next_max = jnp.maximum(run_max, jnp.max(logits, axis=1))
        run_sum = run_sum * jnp.exp(run_max - next_max) + jnp.sum(
            jnp.exp(logits - next_max[:, None]), axis=1
        )
        columns = base_column + block_index * block_width + jnp.arange(block_width, dtype=jnp.int32)
        run_pos = run_pos + jnp.sum(
            jnp.where(columns[None, :] == target_rows[:, None], logits, 0.0), axis=1
        )
        return ((next_max, run_sum, run_pos), None)

    initial = (
        jnp.full((row_count,), -jnp.inf, jnp.float32),
        jnp.zeros((row_count,), jnp.float32),
        jnp.zeros((row_count,), jnp.float32),
    )
    final, _ = lax.scan(
        block_step, initial, (blocks, shifts, jnp.arange(block_count, dtype=jnp.int32))
    )
    return final


def combine(earlier_part, later_part):
    both_max = jnp.maximum(earlier_part[0], later_part[0])
    both_sum = earlier_part[1] * jnp.exp(earlier_part[0] - both_max) + later_part[1] * jnp.exp(
        later_part[0] - both_max
    )
    return (both_max, both_sum, earlier_part[2] + later_part[2])


def add_counts(earlier_part, later_part):
    return earlier_part + later_part


def body(
    tokens, w_hidden, w_out, bank, item_ids, log_freq, positives, new_items, new_owner, queue_head
):
    token_rows = tokens[0]
    pre_act = jnp.dot(
        token_rows,
        lax.all_gather(w_hidden, POOL, axis=0, tiled=True),
        preferred_element_type=jnp.float32,
    )
    hidden = jnp.maximum(pre_act, 0.0).astype(jnp.bfloat16)
    partial_value = jnp.dot(hidden, w_out, preferred_element_type=jnp.float32)
    queries = sum_at_owner(partial_value, "tensor", 0).astype(jnp.bfloat16)
    offsets = jnp.take(log_freq, item_ids).astype(jnp.float32)
    own_index = lax.axis_index(POOL)
    base_column = own_index * bank.shape[0]
    query_piece = lax.all_gather(queries[None], POOL, axis=0, tiled=True)
    target_piece = lax.all_gather(positives, POOL, axis=0, tiled=True)
    groups_in = query_piece.shape[0]
    run_max, run_sum, run_pos = local_stats(
        query_piece.reshape(-1, query_piece.shape[2]),
        target_piece.reshape(-1),
        bank,
        offsets,
        base_column,
    )
    maxima = run_max.reshape(groups_in, -1)
    totals = run_sum.reshape(groups_in, -1)
    scores = run_pos.reshape(groups_in, -1)
    maxima, totals, scores = (maxima, totals, scores)
    maxima, totals, scores = joined_all((maxima, totals, scores), POOL, combine)
    own_max = lax.dynamic_slice_in_dim(maxima, own_index, 1, 0)
    own_sum = lax.dynamic_slice_in_dim(totals, own_index, 1, 0)
    own_pos = lax.dynamic_slice_in_dim(scores, own_index, 1, 0)
    query_loss = own_max + jnp.log(own_sum) - own_pos
    owners = new_owner[:, 0]
    head_slot = queue_head[0]
    shard_rows = bank.shape[0]
    peer_count = lax.axis_size(POOL)
    local_rows = new_items.shape[0]
    capacity = 2 * local_rows // peer_count
    onehot = (owners[:, None] == jnp.arange(peer_count, dtype=jnp.int32)[None, :]).astype(jnp.int32)
    counts = jnp.sum(onehot, axis=0, dtype=jnp.int32)
    before = jnp.sum(
        (jnp.cumsum(onehot, axis=0, dtype=jnp.int32) - onehot) * onehot, axis=1, dtype=jnp.int32
    )
    earlier = entering(counts, POOL, add_counts, jnp.zeros_like(counts))
    ranks = before + jnp.sum(onehot * earlier[None, :], axis=1, dtype=jnp.int32)
    send_pos = owners * capacity + before
    rows_out = (
        jnp.zeros((peer_count * capacity, new_items.shape[1]), jnp.bfloat16)
        .at[send_pos]
        .set(new_items)
    )
    ranks_out = jnp.full((peer_count * capacity,), -1, jnp.int32).at[send_pos].set(ranks)
    rows_in, ranks_in = (
        lax.all_to_all(
            rows_out.reshape(peer_count, capacity, -1),
            POOL,
            split_axis=0,
            concat_axis=0,
            tiled=True,
        ),
        lax.all_to_all(
            ranks_out.reshape(peer_count, capacity), POOL, split_axis=0, concat_axis=0, tiled=True
        ),
    )
    local_slots = jnp.where(ranks_in >= 0, (head_slot + ranks_in) % shard_rows, shard_rows).reshape(
        -1
    )
    new_bank = bank.at[local_slots].set(rows_in.reshape(-1, new_items.shape[1]), mode="drop")
    return (query_loss, new_bank)


def solution(mesh):
    finer = Mesh(
        mesh.devices.reshape(mesh.shape["dp"], mesh.shape["tensor"], 4, 4, 2),
        ("dp", "tensor", "pool_0", "pool_1", "pool_2"),
    )
    in_specs = (
        P(DP_POOL, None, None),
        P(POOL, "tensor"),
        P("tensor", None),
        P(POOL, None),
        P(POOL),
        P(),
        P(DP_POOL, "tensor"),
        P(POOL, None),
        P(POOL, None),
        P(POOL),
    )
    out_specs = (P(DP_POOL, "tensor"), P(POOL, None))
    return jax.shard_map(body, mesh=finer, in_specs=in_specs, out_specs=out_specs, check_vma=False)
```

profile of v0, /device:TPU:1, one launch (start us, length us, event | category | flops | bytes accessed | tf_op | source)
XLA Modules:
  0.0 274.3 jit_solution(2599973721477552642)
XLA Ops:
  7.2 0.7 all-gather.8.cloned.1.call-update
  8.0 74.6 %all-gather.8.cloned.1.call-done = bf16[4096,1024]{1,0:T(8,128)(2,1)} async-done(((bf16[128,1024]{1,0:T(8,128)(2,1)}), bf16[4096,1024]{1,0:T(8,128)(2,1)}) %all-gather.8.cloned.1.call-update) | async-done | bytes 8388624 | tf_op jit(solution)/shard_map/all_gather | solution.py:128
  82.6 16.4 %fusion.12 = f32[1024,256]{1,0:T(8,128)} fusion(bf16[1024,256]{1,0:T(8,128)(2,1)} %param.14, bf16[4096,1024]{1,0:T(8,128)(2,1)} %all-gather.8.cloned.1.call-done, bf16[1,1024,4096]{2,1,0:T(8,128)(2,1)} %param.12), kind=kOutput, calls=%fused_computation.22 | convolution fusion | flops 9128902656 | bytes 18350080 | tf_op jit(solution)/shard_map/dot_general | solution.py:132
  98.9 19.1 %all_to_all.28 = f32[4,256,256]{2,1,0:T(8,128)} all-to-all(f32[4,256,256]{2,1,0:T(8,128)} %bitcast.252), channel_id=1, replica_groups=mesh['dp'=2,'tensor'=4,'pool_0'=4,'pool_1'=4,'pool_2'=2] {'tensor'}, dimensions={0} | all-to-all | bytes 2097152 | tf_op jit(solution)/shard_map/all_to_all | solution.py:19
  118.0 2.0 reduce_sum.56
  120.2 0.6 broadcast_in_dim.52
  120.8 6.5 %all-to-all-start.1 = ((s32[32,1,32]{2,1,0:T(1,128)}), s32[32,1,32]{2,1,0:T(1,128)S(1)}, u32[]{:S(2)}, u32[]{:S(2)}) async-start(s32[32,1,32]{2,1,0:T(1,128)} %broadcast_in_dim.52), calls=%async_computation.1 | async-start | bytes 32768 | tf_op jit(solution)/shard_map/all_to_all | solution.py:51
  127.3 6.8 %gather_fusion = bf16[1024]{0:T(1024)(128)(2,1)S(1)} fusion(bf16[1048576]{0:T(1024)(128)(2,1)S(1)} %copy-done, s32[1024]{0:T(1024)S(1)} %fusion.46), kind=kCustom, calls=%fused_computation | custom fusion | bytes 8192 | tf_op jit(solution)/shard_map/jit(_take)/gather | solution.py:134
  135.4 1.4 scatter_custom_fusion
  136.8 0.7 all_to_all.21
  137.5 7.7 %all-to-all-start.2 = ((s32[32,1,16]{2,1,0:T(1,128)}), s32[32,1,16]{2,1,0:T(1,128)S(1)}, u32[]{:S(2)}, u32[]{:S(2)}) async-start(s32[32,1,16]{2,1,0:T(1,128)} %bitcast.37), calls=%async_computation.2 | async-start | bytes 32768 | tf_op jit(solution)/shard_map/all_to_all | solution.py:184
  145.2 43.7 %all-gather.4 = s32[32,1,256]{2,1,0:T(1,128)S(1)} all-gather(s32[1,1,256]{2,1,0:T(1,128)S(1)} %bitcast.259), channel_id=1, replica_groups=mesh['dp'=2,'tensor'=4,'pool_0'=4,'pool_1'=4,'pool_2'=2] {'pool_0','pool..., dimensions={0}, use_global_device_ids=true | all-gather | bytes 33792 | tf_op jit(solution)/shard_map/all_gather | solution.py:138
  189.6 2.5 scatter_custom_fusion.1
  192.1 3.7 %all-to-all-start.3 = ((bf16[32,16,256]{2,1,0:T(8,128)(2,1)}), bf16[32,16,256]{2,1,0:T(8,128)(2,1)S(1)}, u32[]{:S(2)}, u32[]{:S(2)}) async-start(bf16[32,16,256]{2,1,0:T(8,128)(2,1)} %bitcast.40), calls=%async_computation.3 | async-start | bytes 524288 | tf_op jit(solution)/shard_map/all_to_all | solution.py:177
  196.1 37.4 %while.15 = (s32[]{:T(128)}, f32[8192]{0:T(1024)S(1)}, f32[8192]{0:T(1024)S(1)}, f32[8192]{0:T(1024)S(1)}, bf16[2,512,256]{2,1,0:T(8,128)(2,1)S(1)}, /*index=5*/...) while((s32[]{:T(128)}, f32[8192]{0:T(1024)S(1)}, ...), condition=%wide.region_5.6_spmd.clone, body=%wide.region_1.5_spmd.clone.sunk | while | flops 2181087744 | bytes 38676668 | solution.py:104
  196.2 9.2 %fusion.74 = (f32[8192]{0:T(1024)S(1)}, f32[512,8192]{1,0:T(8,128)}) fusion(f32[512]{0:T(512)S(1)} %bitcast.241, bf16[8192,256]{1,0:T(8,128)(2,1)} %get-tuple-element.234, bf16[2,512,256]{2,1,0:T(8,128)(2,1)S(1)} %get-tuple-element.233, s32[]{:T(128)S(6)} %copy.27), kind=kOutput, calls=%fused_computation.130.clone.1 | convolution fusion | flops 2160058368 | bytes 21268484 | tf_op jit(solution)/shard_map/while/body/eval_jaxpr/dot_general | solution.py:86
  206.7 8.1 %fusion.75 = (f32[8192]{0:T(1024)S(1)}, f32[8192]{0:T(1024)S(1)}) fusion(f32[512,8192]{1,0:T(8,128)} %get-tuple-element.198, s32[8192]{0:T(1024)S(1)} %bitcast.242, s32[512]{0:T(512)S(1)} %iota_add_fusion.2, f32[8192]{0:T(1024)S(1)} %select_maximum_fusion.2), kind=kLoop, calls=%fused_computation.8.clone.1 | loop fusion | flops 20955136 | bytes 16910336 | tf_op jit(solution)/shard_map/while/body/eval_jaxpr/reduce_sum | solution.py:94
  214.8 9.2 %fusion.74 = (f32[8192]{0:T(1024)S(1)}, f32[512,8192]{1,0:T(8,128)}) fusion(f32[512]{0:T(512)S(1)} %bitcast.241, bf16[8192,256]{1,0:T(8,128)(2,1)} %get-tuple-element.234, bf16[2,512,256]{2,1,0:T(8,128)(2,1)S(1)} %get-tuple-element.233, s32[]{:T(128)S(6)} %copy.27), kind=kOutput, calls=%fused_computation.130.clone.1 | convolution fusion | flops 2160058368 | bytes 21268484 | tf_op jit(solution)/shard_map/while/body/eval_jaxpr/dot_general | solution.py:86
  225.3 8.1 %fusion.75 = (f32[8192]{0:T(1024)S(1)}, f32[8192]{0:T(1024)S(1)}) fusion(f32[512,8192]{1,0:T(8,128)} %get-tuple-element.198, s32[8192]{0:T(1024)S(1)} %bitcast.242, s32[512]{0:T(512)S(1)} %iota_add_fusion.2, f32[8192]{0:T(1024)S(1)} %select_maximum_fusion.2), kind=kLoop, calls=%fused_computation.8.clone.1 | loop fusion | flops 20955136 | bytes 16910336 | tf_op jit(solution)/shard_map/while/body/eval_jaxpr/reduce_sum | solution.py:94
  233.6 10.9 %all-gather.1 = f32[384,256]{1,0:T(8,128)S(1)} all-gather(f32[96,256]{1,0:T(8,128)S(1)} %pad_maximum_fusion), channel_id=3, replica_groups=mesh['dp'=2,'tensor'=4,'pool_0'=4,'pool_1'=4,'pool_2'=2] {'pool_0'}, dimensions={0}, use_global_device_ids=true | all-gather | bytes 491520 | tf_op jit(solution)/shard_map/all_gather | solution.py:31
  244.6 11.7 %all-gather.2 = f32[384,256]{1,0:T(8,128)S(1)} all-gather(f32[96,256]{1,0:T(8,128)S(1)} %pad_maximum_fusion.1), channel_id=4, replica_groups=mesh['dp'=2,'tensor'=4,'pool_0'=4,'pool_1'=4,'pool_2'=2] {'pool_1'}, dimensions={0}, use_global_device_ids=true | all-gather | bytes 491520 | tf_op jit(solution)/shard_map/all_gather | solution.py:31
  256.3 7.7 %all-gather.3 = f32[192,256]{1,0:T(8,128)S(1)} all-gather(f32[96,256]{1,0:T(8,128)S(1)} %pad_maximum_fusion.2), channel_id=5, replica_groups=mesh['dp'=2,'tensor'=4,'pool_0'=4,'pool_1'=4,'pool_2'=2] {'pool_2'}, dimensions={0}, use_global_device_ids=true | all-gather | bytes 294912 | tf_op jit(solution)/shard_map/all_gather | solution.py:31
  264.1 2.6 scatter_fusion
  266.7 0.7 fusion.54
  (82 shorter events, 3.4 us)
Async XLA Ops:
  7.2 120.1 %copy-start = (bf16[1048576]{0:T(1024)(128)(2,1)S(1)}, bf16[1048576]{0:T(1024)(128)(2,1)}, u32[]{:S(2)}) copy-start(bf16[1048576]{0:T(1024)(128)(2,1)} %param.17) | copy-start | bytes 6291460
  7.2 75.4 %all-gather.8.cloned.1.call-start = ((), (), s32[]{:S(2)}) async-start(), calls=%async_computation.4 | async-start | bytes 8650752 | tf_op jit(solution)/shard_map/all_gather | solution.py:128
  7.9 112.1 %copy-start.4 = (s32[256,1]{0,1:T(1,128)S(1)}, s32[256,1]{0,1:T(1,128)}, u32[]{:S(2)}) copy-start(s32[256,1]{0,1:T(1,128)} %param.20) | copy-start | bytes 3076
  7.9 119.3 %copy-start.3 = (s32[1024]{0:T(1024)S(1)}, s32[1024]{0:T(1024)}, u32[]{:S(2)}) copy-start(s32[1024]{0:T(1024)} %param.16) | copy-start | bytes 12292
  7.9 137.2 %copy-start.5 = (s32[1,256]{1,0:T(1,128)S(1)}, s32[1,256]{1,0:T(1,128)}, u32[]{:S(2)}) copy-start(s32[1,256]{1,0:T(1,128)} %param.18) | copy-start | bytes 3076
  7.9 188.2 %copy-start.2 = (bf16[1024,256]{1,0:T(8,128)(2,1)S(1)}, bf16[1024,256]{1,0:T(8,128)(2,1)}, u32[]{:S(2)}) copy-start(bf16[1024,256]{1,0:T(8,128)(2,1)} %param.15) | copy-start | bytes 1572868
  8.0 188.2 %all-gather.10.cloned.1.call-start = ((), (), s32[]{:S(2)}) async-start(), calls=%async_computation.5 | async-start | bytes 4325376 | tf_op jit(solution)/shard_map/all_gather | solution.py:137
  120.8 14.2 %all-to-all-start.1 = ((s32[32,1,32]{2,1,0:T(1,128)}), s32[32,1,32]{2,1,0:T(1,128)S(1)}, u32[]{:S(2)}, u32[]{:S(2)}) async-start(s32[32,1,32]{2,1,0:T(1,128)} %broadcast_in_dim.52), calls=%async_computation.1 | async-start | bytes 32768 | tf_op jit(solution)/shard_map/all_to_all | solution.py:51
  137.5 54.6 %all-to-all-start.2 = ((s32[32,1,16]{2,1,0:T(1,128)}), s32[32,1,16]{2,1,0:T(1,128)S(1)}, u32[]{:S(2)}, u32[]{:S(2)}) async-start(s32[32,1,16]{2,1,0:T(1,128)} %bitcast.37), calls=%async_computation.2 | async-start | bytes 32768 | tf_op jit(solution)/shard_map/all_to_all | solution.py:184
  192.1 72.0 %all-to-all-start.3 = ((bf16[32,16,256]{2,1,0:T(8,128)(2,1)}), bf16[32,16,256]{2,1,0:T(8,128)(2,1)S(1)}, u32[]{:S(2)}, u32[]{:S(2)}) async-start(bf16[32,16,256]{2,1,0:T(8,128)(2,1)} %bitcast.40), calls=%async_computation.3 | async-start | bytes 524288 | tf_op jit(solution)/shard_map/all_to_all | solution.py:177
  266.7 0.8 copy-start.1
Sparse Core Ops, SparseCore 0:
  9.8 72.6 all-gather.7
  120.2 60.7 all-gather.9
where the time goes:
time: 275 us; the launch traced here: 274 us
  blocking collectives  93.1 us (34%)
  waiting for transfers between devices  75.3 us (27%)
  matrix products  34.8 us (13%)
  other arithmetic  20.1 us (7%)
  starting transfers between devices  17.9 us (7%)
  local copies, waits for them, and re-layouts  16.6 us (6%)
  between operations  15 us (5%)
    all_gather x1, waiting for transfers between devices, body(): lax.all_gather(w_hidden, POOL, axis=0, tiled=True)  74.6 us
    all_gather x1, blocking collectives, body(): target_piece = lax.all_gather(positives, POOL, axis=0, tiled=True)  43.7 us
    all_gather x3, blocking collectives, all_in_one(): both, at, found = (lax.all_gather(jnp.concatenate(lines), axis), 0, {})  30.3 us
    all_to_all x1, blocking collectives, sum_at_owner(): blocks = lax.all_to_all(split_up(x, dim, count), axis, 0, 0, tiled=True)  19.1 us
    dot_general x2, matrix products, block_step(): jnp.dot(query_rows, bank_block.T, preferred_element_type=jnp.float32)  18.5 us
    dot_general x1, matrix products, body(): partial_value = jnp.dot(hidden, w_out, preferred_element_type=jnp.float32)  16.4 us
    reduce_sum x2, other arithmetic, block_step(): jnp.sum(jnp.where(columns[None, :] == target_rows[:, None], logits, 0.0),...  16.2 us
    all_to_all x1, starting transfers between devices, body(): lax.all_to_all(ranks_out.reshape(peer_count, capacity), POOL, split_axis=...  7.69 us
  transfers between devices with their start and end apart: 5, of which 1 were waited for; matrix products, arithmetic and copies ran while one was open for 18% of the time, Pallas kernels for 0%

commit v1 on v0

--- a/solution.py
+++ b/solution.py
@@ -135,7 +135,9 @@
     own_index = lax.axis_index(POOL)
     base_column = own_index * bank.shape[0]
     query_piece = lax.all_gather(queries[None], POOL, axis=0, tiled=True)
-    target_piece = lax.all_gather(positives, POOL, axis=0, tiled=True)
+    target_piece = jnp.concatenate(
+        lax.all_to_all(jnp.stack([positives] * lax.axis_size(POOL)), POOL, 0, 0), axis=0
+    )
     groups_in = query_piece.shape[0]
     run_max, run_sum, run_pos = local_stats(
         query_piece.reshape(-1, query_piece.shape[2]),

time: 275 us -> 261 us (0.949)
  blocking collectives: 93.1 us -> 48.1 us
  waiting for transfers between devices: 75.3 us -> 101 us
  starting transfers between devices: 17.9 us -> 22.6 us
    all_gather x1 -> x0, blocking collectives: 43.7 us -> none  [body(): target_piece = lax.all_gather(positives, POOL, axis=0, tiled=True)]
    all_gather x1, waiting for transfers between devices: 0.02 us -> 14.4 us  [body(): query_piece = lax.all_gather(queries[None], POOL, axis=0, tiled=True)]
    all_to_all x0 -> x1, waiting for transfers between devices: none -> 7.47 us  [body(): lax.all_to_all(jnp.stack([positives] * lax.axis_size(POOL)), POOL, 0, 0)]
    all_to_all x0 -> x1, starting transfers between devices: none -> 4.42 us  [body(): lax.all_to_all(jnp.stack([positives] * lax.axis_size(POOL)), POOL, 0, 0)]
    all_to_all x1, waiting for transfers between devices: 0.01 us -> 4.03 us  [body(): lax.all_to_all(ranks_out.reshape(peer_count, capacity), POOL, split_axis=...]
  transfers between devices with their start and end apart: 5 -> 6, of which waited for: 1 -> 4; matrix products, arithmetic and copies ran while one was open for 18% -> 19% of each run, Pallas kernels for 0% -> 0%
where the time goes in v1:
time: 261 us; the launch traced here: 260 us
  waiting for transfers between devices  101 us (39%)
  blocking collectives  48.1 us (18%)
  matrix products  34.8 us (13%)
  starting transfers between devices  22.6 us (9%)
  other arithmetic  20.1 us (8%)
  local copies, waits for them, and re-layouts  17.2 us (7%)
  between operations  15 us (6%)
    all_gather x1, waiting for transfers between devices, body(): lax.all_gather(w_hidden, POOL, axis=0, tiled=True)  74.6 us
    all_gather x3, blocking collectives, all_in_one(): both, at, found = (lax.all_gather(jnp.concatenate(lines), axis), 0, {})  29.1 us
    all_to_all x1, blocking collectives, sum_at_owner(): blocks = lax.all_to_all(split_up(x, dim, count), axis, 0, 0, tiled=True)  19.1 us
    dot_general x2, matrix products, block_step(): jnp.dot(query_rows, bank_block.T, preferred_element_type=jnp.float32)  18.5 us
    dot_general x1, matrix products, body(): partial_value = jnp.dot(hidden, w_out, preferred_element_type=jnp.float32)  16.4 us
    reduce_sum x2, other arithmetic, block_step(): jnp.sum(jnp.where(columns[None, :] == target_rows[:, None], logits, 0.0),...  16.2 us
    all_gather x1, waiting for transfers between devices, body(): query_piece = lax.all_gather(queries[None], POOL, axis=0, tiled=True)  14.4 us
    all_to_all x1, starting transfers between devices, body(): lax.all_to_all(ranks_out.reshape(peer_count, capacity), POOL, split_axis=...  7.69 us
  transfers between devices with their start and end apart: 6, of which 4 were waited for; matrix products, arithmetic and copies ran while one was open for 19% of the time, Pallas kernels for 0%

profile of v1, /device:TPU:1, one launch (start us, length us, event | category | flops | bytes accessed | tf_op | source)
XLA Modules:
  0.0 260.4 jit_solution(15884594271014106948)
XLA Ops:
  7.2 0.7 all-gather.7.cloned.1.call-update
  8.0 74.6 %all-gather.7.cloned.1.call-done = bf16[4096,1024]{1,0:T(8,128)(2,1)} async-done(((bf16[128,1024]{1,0:T(8,128)(2,1)}), bf16[4096,1024]{1,0:T(8,128)(2,1)}) %all-gather.7.cloned.1.call-update) | async-done | bytes 8388624 | tf_op jit(solution)/shard_map/all_gather | solution.py:128
  82.6 16.4 %fusion.12 = f32[1024,256]{1,0:T(8,128)} fusion(bf16[1024,256]{1,0:T(8,128)(2,1)} %param.14, bf16[4096,1024]{1,0:T(8,128)(2,1)} %all-gather.7.cloned.1.call-done, bf16[1,1024,4096]{2,1,0:T(8,128)(2,1)} %param.12), kind=kOutput, calls=%fused_computation.22 | convolution fusion | flops 9128902656 | bytes 18350080 | tf_op jit(solution)/shard_map/dot_general | solution.py:132
  98.9 19.1 %all_to_all.33 = f32[4,256,256]{2,1,0:T(8,128)} all-to-all(f32[4,256,256]{2,1,0:T(8,128)} %bitcast.244), channel_id=1, replica_groups=mesh['dp'=2,'tensor'=4,'pool_0'=4,'pool_1'=4,'pool_2'=2] {'tensor'}, dimensions={0} | all-to-all | bytes 2097152 | tf_op jit(solution)/shard_map/all_to_all | solution.py:19
  118.0 2.0 reduce_sum.56
  120.8 6.5 %all-to-all-start.2 = ((s32[32,1,32]{2,1,0:T(1,128)}), s32[32,1,32]{2,1,0:T(1,128)S(1)}, u32[]{:S(2)}, u32[]{:S(2)}) async-start(s32[32,1,32]{2,1,0:T(1,128)} %broadcast_in_dim.52), calls=%async_computation.2 | async-start | bytes 32768 | tf_op jit(solution)/shard_map/all_to_all | solution.py:51
  128.1 6.8 %gather_fusion = bf16[1024]{0:T(1024)(128)(2,1)S(1)} fusion(bf16[1048576]{0:T(1024)(128)(2,1)S(1)} %copy-done, s32[1024]{0:T(1024)S(1)} %fusion.46), kind=kCustom, calls=%fused_computation | custom fusion | bytes 8192 | tf_op jit(solution)/shard_map/jit(_take)/gather | solution.py:134
  135.4 1.4 scatter_custom_fusion
  137.4 7.7 %all-to-all-start.3 = ((s32[32,1,16]{2,1,0:T(1,128)}), s32[32,1,16]{2,1,0:T(1,128)S(1)}, u32[]{:S(2)}, u32[]{:S(2)}) async-start(s32[32,1,16]{2,1,0:T(1,128)} %bitcast.37), calls=%async_computation.3 | async-start | bytes 32768 | tf_op jit(solution)/shard_map/all_to_all | solution.py:186
  145.8 2.5 scatter_custom_fusion.1
  148.3 4.0 %all-to-all-done.3 = s32[32,1,16]{2,1,0:T(1,128)S(1)} async-done(((s32[32,1,16]{2,1,0:T(1,128)}), s32[32,1,16]{2,1,0:T(1,128)S(1)}, u32[]{:S(2)}, u32[]{:S(2)}) %all-to-all-start.3) | async-done | bytes 2080 | tf_op jit(solution)/shard_map/all_to_all | solution.py:186
  153.0 4.4 %all-to-all-start.1 = ((s32[32,1,256]{2,1,0:T(1,128)}), s32[32,1,256]{2,1,0:T(1,128)S(1)}, u32[]{:S(2)}, u32[]{:S(2)}) async-start(s32[32,1,256]{2,1,0:T(1,128)} %stack.2), calls=%async_computation.1 | async-start | bytes 65536 | tf_op jit(solution)/shard_map/all_to_all | solution.py:139
  157.7 7.5 %all-to-all-done.1 = s32[32,1,256]{2,1,0:T(1,128)S(1)} async-done(((s32[32,1,256]{2,1,0:T(1,128)}), s32[32,1,256]{2,1,0:T(1,128)S(1)}, u32[]{:S(2)}, u32[]{:S(2)}) %all-to-all-start.1) | async-done | bytes 32800 | tf_op jit(solution)/shard_map/all_to_all | solution.py:139
  165.2 3.9 %all-to-all-start.4 = ((bf16[32,16,256]{2,1,0:T(8,128)(2,1)}), bf16[32,16,256]{2,1,0:T(8,128)(2,1)S(1)}, u32[]{:S(2)}, u32[]{:S(2)}) async-start(bf16[32,16,256]{2,1,0:T(8,128)(2,1)} %bitcast.40), calls=%async_computation.4 | async-start | bytes 524288 | tf_op jit(solution)/shard_map/all_to_all | solution.py:179
  169.1 14.4 %all-gather.9.cloned.1.call-done = bf16[8192,256]{1,0:T(8,128)(2,1)} async-done(((bf16[256,256]{1,0:T(8,128)(2,1)}), bf16[8192,256]{1,0:T(8,128)(2,1)}) %all-gather.9.cloned.1.call-update) | async-done | bytes 4194320 | tf_op jit(solution)/shard_map/all_gather | solution.py:137
  183.6 37.3 %while.15 = (s32[]{:T(128)}, f32[8192]{0:T(1024)S(1)}, f32[8192]{0:T(1024)S(1)}, f32[8192]{0:T(1024)S(1)}, bf16[2,512,256]{2,1,0:T(8,128)(2,1)S(1)}, /*index=5*/...) while((s32[]{:T(128)}, f32[8192]{0:T(1024)S(1)}, ...), condition=%wide.region_5.6_spmd.clone, body=%wide.region_1.5_spmd.clone.sunk | while | flops 2181087744 | bytes 38611132 | solution.py:104
  183.6 9.2 %fusion.74 = (f32[8192]{0:T(1024)S(1)}, f32[512,8192]{1,0:T(8,128)}) fusion(f32[512]{0:T(512)S(1)} %bitcast.235, bf16[8192,256]{1,0:T(8,128)(2,1)} %get-tuple-element.234, bf16[2,512,256]{2,1,0:T(8,128)(2,1)S(1)} %get-tuple-element.233, s32[]{:T(128)S(6)} %copy.21), kind=kOutput, calls=%fused_computation.129.clone.1 | convolution fusion | flops 2160058368 | bytes 21268484 | tf_op jit(solution)/shard_map/while/body/eval_jaxpr/dot_general | solution.py:86
  194.0 8.1 %fusion.75 = (f32[8192]{0:T(1024)S(1)}, f32[8192]{0:T(1024)S(1)}) fusion(f32[512,8192]{1,0:T(8,128)} %get-tuple-element.198, s32[8192]{0:T(1024)S(1)} %bitcast.240, s32[512]{0:T(512)S(1)} %iota_add_fusion.2, f32[8192]{0:T(1024)S(1)} %select_maximum_fusion.2), kind=kLoop, calls=%fused_computation.8.clone.1 | loop fusion | flops 20955136 | bytes 16910336 | tf_op jit(solution)/shard_map/while/body/eval_jaxpr/reduce_sum | solution.py:94
  202.2 9.2 %fusion.74 = (f32[8192]{0:T(1024)S(1)}, f32[512,8192]{1,0:T(8,128)}) fusion(f32[512]{0:T(512)S(1)} %bitcast.235, bf16[8192,256]{1,0:T(8,128)(2,1)} %get-tuple-element.234, bf16[2,512,256]{2,1,0:T(8,128)(2,1)S(1)} %get-tuple-element.233, s32[]{:T(128)S(6)} %copy.21), kind=kOutput, calls=%fused_computation.129.clone.1 | convolution fusion | flops 2160058368 | bytes 21268484 | tf_op jit(solution)/shard_map/while/body/eval_jaxpr/dot_general | solution.py:86
  212.7 8.1 %fusion.75 = (f32[8192]{0:T(1024)S(1)}, f32[8192]{0:T(1024)S(1)}) fusion(f32[512,8192]{1,0:T(8,128)} %get-tuple-element.198, s32[8192]{0:T(1024)S(1)} %bitcast.240, s32[512]{0:T(512)S(1)} %iota_add_fusion.2, f32[8192]{0:T(1024)S(1)} %select_maximum_fusion.2), kind=kLoop, calls=%fused_computation.8.clone.1 | loop fusion | flops 20955136 | bytes 16910336 | tf_op jit(solution)/shard_map/while/body/eval_jaxpr/reduce_sum | solution.py:94
  220.9 9.6 %all-gather.1 = f32[384,256]{1,0:T(8,128)S(1)} all-gather(f32[96,256]{1,0:T(8,128)S(1)} %pad_maximum_fusion), channel_id=3, replica_groups=mesh['dp'=2,'tensor'=4,'pool_0'=4,'pool_1'=4,'pool_2'=2] {'pool_0'}, dimensions={0}, use_global_device_ids=true | all-gather | bytes 491520 | tf_op jit(solution)/shard_map/all_gather | solution.py:31
  230.6 11.8 %all-gather.2 = f32[384,256]{1,0:T(8,128)S(1)} all-gather(f32[96,256]{1,0:T(8,128)S(1)} %pad_maximum_fusion.1), channel_id=4, replica_groups=mesh['dp'=2,'tensor'=4,'pool_0'=4,'pool_1'=4,'pool_2'=2] {'pool_1'}, dimensions={0}, use_global_device_ids=true | all-gather | bytes 491520 | tf_op jit(solution)/shard_map/all_gather | solution.py:31
  242.5 7.6 %all-gather.3 = f32[192,256]{1,0:T(8,128)S(1)} all-gather(f32[96,256]{1,0:T(8,128)S(1)} %pad_maximum_fusion.2), channel_id=5, replica_groups=mesh['dp'=2,'tensor'=4,'pool_0'=4,'pool_1'=4,'pool_2'=2] {'pool_2'}, dimensions={0}, use_global_device_ids=true | all-gather | bytes 294912 | tf_op jit(solution)/shard_map/all_gather | solution.py:31
  250.2 2.6 %scatter_fusion = bf16[1024,256]{1,0:T(8,128)(2,1)S(1)} fusion(bf16[1024,256]{1,0:T(8,128)(2,1)S(1)} %bitcast.233, s32[512]{0:T(512)S(1)} %bitcast.250, bf16[512,256]{1,0:T(8,128)(2,1)S(1)} %bitcast.243), kind=kCustom, calls=%fused_computation.3 | custom fusion | bytes 788480 | tf_op jit(solution)/shard_map/scatter | solution.py:193
  (81 shorter events, 5.9 us)
Async XLA Ops:
  7.2 121.0 %copy-start = (bf16[1048576]{0:T(1024)(128)(2,1)S(1)}, bf16[1048576]{0:T(1024)(128)(2,1)}, u32[]{:S(2)}) copy-start(bf16[1048576]{0:T(1024)(128)(2,1)} %param.17) | copy-start | bytes 6291460
  7.2 75.4 %all-gather.7.cloned.1.call-start = ((), (), s32[]{:S(2)}) async-start(), calls=%async_computation.5 | async-start | bytes 8650752 | tf_op jit(solution)/shard_map/all_gather | solution.py:128
  7.9 112.1 %copy-start.4 = (s32[256,1]{0,1:T(1,128)S(1)}, s32[256,1]{0,1:T(1,128)}, u32[]{:S(2)}) copy-start(s32[256,1]{0,1:T(1,128)} %param.20) | copy-start | bytes 3076
  7.9 120.1 %copy-start.3 = (s32[1024]{0:T(1024)S(1)}, s32[1024]{0:T(1024)}, u32[]{:S(2)}) copy-start(s32[1024]{0:T(1024)} %param.16) | copy-start | bytes 12292
  7.9 144.4 %copy-start.5 = (s32[1,256]{1,0:T(1,128)S(1)}, s32[1,256]{1,0:T(1,128)}, u32[]{:S(2)}) copy-start(s32[1,256]{1,0:T(1,128)} %param.18) | copy-start | bytes 3076
  7.9 175.6 %copy-start.2 = (bf16[1024,256]{1,0:T(8,128)(2,1)S(1)}, bf16[1024,256]{1,0:T(8,128)(2,1)}, u32[]{:S(2)}) copy-start(bf16[1024,256]{1,0:T(8,128)(2,1)} %param.15) | copy-start | bytes 1572868
  8.0 175.6 %all-gather.9.cloned.1.call-start = ((), (), s32[]{:S(2)}) async-start(), calls=%async_computation.6 | async-start | bytes 4325376 | tf_op jit(solution)/shard_map/all_gather | solution.py:137
  120.8 14.2 %all-to-all-start.2 = ((s32[32,1,32]{2,1,0:T(1,128)}), s32[32,1,32]{2,1,0:T(1,128)S(1)}, u32[]{:S(2)}, u32[]{:S(2)}) async-start(s32[32,1,32]{2,1,0:T(1,128)} %broadcast_in_dim.52), calls=%async_computation.2 | async-start | bytes 32768 | tf_op jit(solution)/shard_map/all_to_all | solution.py:51
  137.4 14.9 %all-to-all-start.3 = ((s32[32,1,16]{2,1,0:T(1,128)}), s32[32,1,16]{2,1,0:T(1,128)S(1)}, u32[]{:S(2)}, u32[]{:S(2)}) async-start(s32[32,1,16]{2,1,0:T(1,128)} %bitcast.37), calls=%async_computation.3 | async-start | bytes 32768 | tf_op jit(solution)/shard_map/all_to_all | solution.py:186
  153.0 12.2 %all-to-all-start.1 = ((s32[32,1,256]{2,1,0:T(1,128)}), s32[32,1,256]{2,1,0:T(1,128)S(1)}, u32[]{:S(2)}, u32[]{:S(2)}) async-start(s32[32,1,256]{2,1,0:T(1,128)} %stack.2), calls=%async_computation.1 | async-start | bytes 65536 | tf_op jit(solution)/shard_map/all_to_all | solution.py:139
  165.2 85.0 %all-to-all-start.4 = ((bf16[32,16,256]{2,1,0:T(8,128)(2,1)}), bf16[32,16,256]{2,1,0:T(8,128)(2,1)S(1)}, u32[]{:S(2)}, u32[]{:S(2)}) async-start(bf16[32,16,256]{2,1,0:T(8,128)(2,1)} %bitcast.40), calls=%async_computation.4 | async-start | bytes 524288 | tf_op jit(solution)/shard_map/all_to_all | solution.py:179
  252.8 0.8 copy-start.1
Sparse Core Ops, SparseCore 0:
  9.8 72.6 all-gather.6
  120.2 63.3 all-gather.8
